TPU v7x, 128 devices: a whole 4x4x4 slice. The times are simulated.
128 devices in a mesh: chan: 8 (over y, core), inp: 16 (over z, x).
Axes of the slice: x: 4, y: 4, z: 4, core: 2. Of those that a mesh axis runs over, the one named last changes fastest.
Arguments:
- voltages: bfloat16 [1024, 262144], P('inp', 'chan'), may hold values from -64 to 64
- tile_table: int32 [144, 2], replicated, may hold values from -1 to 15, as said below
Outputs:
- coherence: float32 [512, 144, 64, 128], P('chan', 'inp')
Inputs may be any that keep to these rules, and one draw needn't show every extreme that they name: `tile_table`: rows 9 d to 9 d + 8 are the slots whose tiles the device at index d along inp outputs. Every pair (a, b) with 0 <= a <= b < 16 stands in exactly one row, and every other row is (-1, -1); the pairs are spread over the rows in any order.
All inputs are finite; a program needn't handle non-finite values.
Results may differ from a plain program's by a relative error of at most 0.0058.
Values may be sent and summed in bfloat16 or wider, within the bound.
No kernel may reach another device: no remote copies, remote signals or barrier semaphores. Data moves between devices by JAX's collectives and lax.ppermute only.
A program may use at most 128 MiB of HBM per device.

v0:
```python
import math
import jax
import jax.numpy as jnp
from jax import lax
from jax.sharding import Mesh
from jax.sharding import PartitionSpec as P

L = 2048
NCH = 512
TAPS = 4
CHAN = ("chan_0", "chan_1")


def passed_along(array, axis, by):
    devices = lax.axis_size(axis)
    pairs = [(i, i + by) for i in range(devices) if 0 <= i + by < devices]
    return lax.ppermute(array, axis, pairs)


def in_blocks(array, dim, devices):
    before, after = (array.shape[:dim], array.shape[dim + 1 :])
    return jnp.moveaxis(array.reshape(*before, devices, -1, *after), dim, 0)


def laid_out(parts, dim):
    parts = jnp.moveaxis(parts, 0, dim)
    shape = parts.shape
    return parts.reshape(*shape[:dim], shape[dim] * shape[dim + 1], *shape[dim + 2 :])


def exchange_in_order(parts, axes, order):
    inside = parts.shape[1:]
    whole = parts.reshape(*(lax.axis_size(a) for a in axes), *inside)
    for k in order:
        whole = lax.all_to_all(whole, axes[k], k, k, tiled=True)
    return whole.reshape(-1, *inside)


def core_and_chips(array, groups, order, split_dim, concat_dim):
    devices = lax.axis_size(groups[0]) * lax.axis_size(groups[1])
    parts = in_blocks(array, split_dim, devices)
    return laid_out(exchange_in_order(parts, groups, order), concat_dim)


def filter_window():
    positions = jnp.arange(TAPS * L, dtype=jnp.float32)
    shape_sinc = jnp.sinc((positions - TAPS * L / 2.0) / L)
    tapering = 0.5 - 0.5 * jnp.cos(2.0 * math.pi * positions / (TAPS * L))
    return (shape_sinc * tapering).reshape(TAPS, L)


def transform_table():
    samples = jnp.arange(L, dtype=jnp.int32)[:, None]
    channels = jnp.arange(NCH, dtype=jnp.int32)[None, :]
    phases = samples * channels % L
    angles = phases.astype(jnp.float32) * (2.0 * math.pi / L)
    return (
        jnp.stack([jnp.cos(angles), -jnp.sin(angles)], axis=2)
        .reshape(L, 2 * NCH)
        .astype(jnp.bfloat16)
    )


def rotate_parts(rows):
    half_width = rows.shape[-1] // 2
    return jnp.concatenate([-rows[..., half_width:], rows[..., :half_width]], axis=-1)


def arrange(turned):
    input_count, frame_total, column_count = turned.shape
    return (
        turned.reshape(input_count, frame_total, column_count // 2, 2)
        .transpose(2, 0, 3, 1)
        .reshape(column_count // 2, input_count, 2 * frame_total)
    )


def channelize(voltages):
    block_width, local_len = voltages.shape
    local_frames = local_len // L
    blocks = voltages.reshape(block_width, local_frames, L)
    following = passed_along(blocks[:, : TAPS - 1, :], CHAN, -1)
    extended = jnp.concatenate([blocks, following], axis=1)
    window = filter_window()
    filtered = jnp.zeros((block_width, local_frames, L), jnp.float32)
    for tap_index in range(TAPS):
        filtered = (
            filtered
            + extended[:, tap_index : tap_index + local_frames, :].astype(jnp.float32)
            * window[tap_index]
        )
    filtered = filtered.astype(jnp.bfloat16).reshape(block_width * local_frames, L)
    spectra = jnp.dot(filtered, transform_table(), preferred_element_type=jnp.float32).astype(
        jnp.bfloat16
    )
    return spectra.reshape(block_width, local_frames, 2 * NCH)


def make_tile(everything, autopower, row_block, col_block, block_width, frame_total):
    present = (row_block >= 0).astype(jnp.float32)
    first = jnp.maximum(row_block, 0)
    second = jnp.maximum(col_block, 0)
    left_rows = lax.dynamic_slice_in_dim(everything, first * block_width, block_width, 1)
    right_rows = lax.dynamic_slice_in_dim(everything, second * block_width, block_width, 1)
    partner = jnp.concatenate([right_rows, rotate_parts(right_rows)], axis=1)
    product = jnp.einsum("cif,cjf->cij", left_rows, partner, preferred_element_type=jnp.float32)
    power_left = lax.dynamic_slice_in_dim(autopower, first * block_width, block_width, 1)
    power_right = lax.dynamic_slice_in_dim(autopower, second * block_width, block_width, 1)
    inverse = present / (frame_total * jnp.sqrt(power_left[:, :, None] * power_right[:, None, :]))
    return product * jnp.concatenate([inverse, inverse], axis=2)


def on_device(voltages, tile_table):
    block_width = voltages.shape[0]
    spectra = channelize(voltages)
    turned = core_and_chips(spectra, ("chan_0", "chan_1"), (1, 0), 2, 1)
    own = arrange(turned)
    everything = lax.all_gather(own, "inp", axis=1, tiled=True)
    frame_total = everything.shape[2] // 2
    autopower = jnp.sum(jnp.square(everything.astype(jnp.float32)), axis=2) / frame_total + 1e-06
    slot_total = tile_table.shape[0] // lax.axis_size("inp")
    device_index = lax.axis_index("inp")
    slot_rows = lax.dynamic_slice_in_dim(tile_table, device_index * slot_total, slot_total, 0)
    outputs = jnp.zeros(
        (everything.shape[0], slot_total, block_width, 2 * block_width), jnp.float32
    )

    def place(slot_index, current):
        tile_out = make_tile(
            everything,
            autopower,
            slot_rows[slot_index, 0],
            slot_rows[slot_index, 1],
            block_width,
            frame_total,
        )
        return lax.dynamic_update_index_in_dim(current, tile_out, slot_index, 1)

    return lax.fori_loop(0, slot_total, place, outputs)


def solution(mesh):
    torus = Mesh(mesh.devices.reshape(4, 2, mesh.shape["inp"]), ("chan_0", "chan_1", "inp"))
    placed = (P("inp", CHAN), P())
    return jax.shard_map(
        on_device,
        mesh=torus,
        in_specs=placed,
        out_specs=P(CHAN, "inp", None, None),
        check_vma=False,
    )
```

profile of v0, /device:TPU:1, one launch (start us, length us, event | category | flops | bytes accessed | tf_op | source)
XLA Modules:
  0.0 443.4 jit_solution(10876512019919204436)
XLA Ops:
  6.5 4.6 %copy.31 = bf16[8,8,16,2048]{3,2,1,0:T(8,128)(2,1)S(1)} copy(bf16[8,8,16,2048]{3,1,2,0:T(8,128)(2,1)} %bitcast.47) | data formatting | bytes 8388608
  11.2 2.0 copy-done.2
  14.3 3.5 collective-permute-start
  17.8 17.1 %negate_convert_fusion = (bf16[2048,512,1]{1,0,2:T(8,128)(2,1)S(1)}, bf16[2048,512,1]{1,0,2:T(8,128)(2,1)S(1)}) fusion(), kind=kLoop, calls=%fused_computation.29 | loop fusion | flops 17825792 | bytes 4194304 | tf_op jit(solution)/shard_map/convert.2
  34.9 2.3 pad_maximum_fusion
  37.2 11.3 %copy.21 = bf16[2048,512,2]{0,2,1:T(2,128)(2,1)} copy(bf16[2048,512,2]{1,0,2:T(8,128)(2,1)} %pad_maximum_fusion) | data formatting | bytes 8388608 | tf_op jit(solution)/shard_map/stack | solution.py:58
  48.6 7.3 %convert_element_type.68 = bf16[2048,1024]{0,1:T(8,128)(2,1)} reshape(bf16[2048,512,2]{0,2,1:T(2,128)(2,1)} %copy.21) | data formatting | bytes 8388608 | tf_op jit(solution)/shard_map/convert_element_type | solution.py:60
  56.0 2.7 constant_dynamic-update-slice_fusion
  58.7 1.0 copy_dynamic-update-slice_fusion
  59.8 5.0 %add_convert_fusion = bf16[64,16,2048]{2,1,0:T(8,128)(2,1)S(1)} fusion(bf16[64,19,2048]{2,1,0:T(8,128)(2,1)S(1)} %copy_dynamic-update-slice_fusion, f32[2048]{0:T(1024)S(1)} %get-tuple-element.117, f32[2048]{0:T(1024)S(1)} %get-tuple-element.118, f32[2048]{0:T(1024)S(1)} %get-tuple-element.119, f32[2048]{0:T(1024)S(1)} %get-tuple-element.116, ...), kind=kLoop, calls=%fused_computation.21 | loop fusion | flops 25165824 | bytes 21004288 | tf_op jit(solution)/shard_map/convert_element_type | solution.py:92
  64.7 4.8 %convert_bitcast_fusion = bf16[128,8,8,128]{3,1,2,0:T(8,128)(2,1)S(1)} fusion(bf16[1024,2048]{1,0:T(8,128)(2,1)S(1)} %bitcast.46, bf16[2048,1024]{0,1:T(8,128)(2,1)S(1)} %copy-done.4), kind=kOutput, calls=%fused_computation.34 | convolution fusion | flops 4296015872 | bytes 10485760 | tf_op jit(solution)/shard_map/dot_general | solution.py:93
  69.5 0.6 copy.32
  70.8 5.1 %all_to_all.10 = bf16[4,2,64,16,128]{4,3,2,0,1:T(8,128)(2,1)S(1)} all-to-all(bf16[4,2,64,16,128]{4,3,2,0,1:T(8,128)(2,1)S(1)} %copy.23), channel_id=1, replica_groups=mesh['chan_0'=4,'chan_1'=2,'inp'=16] {'chan_1'}, dimensions={1} | all-to-all | bytes 4194304 | tf_op jit(solution)/shard_map/all_to_all | solution.py:35
  76.2 29.6 %all_to_all.11 = bf16[4,2,64,16,128]{4,3,2,1,0:T(8,128)(2,1)S(1)} all-to-all(bf16[4,2,64,16,128]{4,3,2,1,0:T(8,128)(2,1)S(1)} %copy.24), channel_id=1, replica_groups=mesh['chan_0'=4,'chan_1'=2,'inp'=16] {'chan_0'}, dimensions={0} | all-to-all | bytes 4194304 | tf_op jit(solution)/shard_map/all_to_all | solution.py:35
  105.8 7.4 %copy.25 = bf16[8,64,16,128]{1,2,0,3:T(8,128)(2,1)} copy(bf16[8,64,16,128]{3,2,1,0:T(8,128)(2,1)S(1)} %bitcast.43) | data formatting | bytes 4194304 | tf_op jit(solution)/shard_map/reshape | solution.py:36
  113.1 4.8 %copy.26 = bf16[64,64,256]{2,1,0:T(8,128)(2,1)} copy(bf16[64,64,256]{1,2,0:T(8,128)(2,1)} %bitcast.42) | data formatting | bytes 4194304 | tf_op jit(solution)/shard_map/reshape | solution.py:74
  118.0 198.5 %all-gather.2.cloned.1.call-done = bf16[64,1024,256]{2,1,0:T(8,128)(2,1)} async-done(((bf16[64,64,256]{2,1,0:T(8,128)(2,1)}), bf16[64,1024,256]{2,1,0:T(8,128)(2,1)}) %all-gather.2.cloned.1.call-update) | async-done | bytes 33554448 | tf_op jit(solution)/shard_map/all_gather | solution.py:118
  316.5 11.9 %multiply_reduce_fusion = f32[64,1024]{1,0:T(8,128)S(1)} fusion(bf16[64,1024,256]{2,1,0:T(8,128)(2,1)} %all-gather.2.cloned.1.call-done), kind=kLoop, calls=%fused_computation.20 | loop fusion | flops 50266112 | bytes 33816576 | tf_op jit(solution)/shard_map/reduce_sum | solution.py:120
  328.4 107.4 %while.13 = (s32[]{:T(128)}, f32[64,9,64,128]{3,2,1,0:T(8,128)}, s32[9,2]{0,1:T(2,128)S(1)}, bf16[64,1024,256]{2,1,0:T(8,128)(2,1)}, f32[64,1024]{1,0:T(8,128)S(...) while((s32[]{:T(128)}, f32[64,9,64,128]{3,2,1,0:T(8,128)}, ...), condition=%wide.region_2.3_spmd, body=%wide.region_1.2_spmd.sunk | while | flops 284426240 | bytes 18973484 | solution.py:139
  328.4 0.6 constant_dynamic-slice_fusion.10
  331.1 0.8 multiply_divide_fusion.2
  331.9 2.1 dynamic-slice_negate_fusion.2
  334.0 1.7 constant_dynamic-slice_fusion.12
  335.8 4.6 %fusion.57 = f32[64,9,64,128]{3,2,1,0:T(8,128)} fusion(f32[64,9,64,128]{3,2,1,0:T(8,128)} %get-tuple-element.177, s32[]{:T(128)} %get-tuple-element.176, f32[64,64,64]{2,1,0:T(8,128)S(1)} %multiply_divide_fusion.2, bf16[64,64,128]{2,1,0:T(8,128)(2,1)S(1)} %get-tuple-element.163, bf16[64,64,128]{2,1,0:T(8,128)(2,1)S(1)} %get-tuple-element.164, ...), kind=kOutput, calls=%fused_computation.8.clone.1 | convolution fusion | flops 282066944 | bytes 9437700 | tf_op jit(solution)/shard_map/while/body/eval_jaxpr/cif,cjf->cij/dot_general | solution.py:106
  340.4 0.6 constant_dynamic-slice_fusion.10
  343.0 0.8 multiply_divide_fusion.2
  343.8 2.1 dynamic-slice_negate_fusion.2
  345.9 1.7 constant_dynamic-slice_fusion.12
  347.7 4.6 %fusion.57 = f32[64,9,64,128]{3,2,1,0:T(8,128)} fusion(f32[64,9,64,128]{3,2,1,0:T(8,128)} %get-tuple-element.177, s32[]{:T(128)} %get-tuple-element.176, f32[64,64,64]{2,1,0:T(8,128)S(1)} %multiply_divide_fusion.2, bf16[64,64,128]{2,1,0:T(8,128)(2,1)S(1)} %get-tuple-element.163, bf16[64,64,128]{2,1,0:T(8,128)(2,1)S(1)} %get-tuple-element.164, ...), kind=kOutput, calls=%fused_computation.8.clone.1 | convolution fusion | flops 282066944 | bytes 9437700 | tf_op jit(solution)/shard_map/while/body/eval_jaxpr/cif,cjf->cij/dot_general | solution.py:106
  352.3 0.6 constant_dynamic-slice_fusion.10
  354.9 0.8 multiply_divide_fusion.2
  355.8 2.1 dynamic-slice_negate_fusion.2
  357.9 1.7 constant_dynamic-slice_fusion.12
  359.6 4.6 %fusion.57 = f32[64,9,64,128]{3,2,1,0:T(8,128)} fusion(f32[64,9,64,128]{3,2,1,0:T(8,128)} %get-tuple-element.177, s32[]{:T(128)} %get-tuple-element.176, f32[64,64,64]{2,1,0:T(8,128)S(1)} %multiply_divide_fusion.2, bf16[64,64,128]{2,1,0:T(8,128)(2,1)S(1)} %get-tuple-element.163, bf16[64,64,128]{2,1,0:T(8,128)(2,1)S(1)} %get-tuple-element.164, ...), kind=kOutput, calls=%fused_computation.8.clone.1 | convolution fusion | flops 282066944 | bytes 9437700 | tf_op jit(solution)/shard_map/while/body/eval_jaxpr/cif,cjf->cij/dot_general | solution.py:106
  364.2 0.6 constant_dynamic-slice_fusion.10
  366.9 0.8 multiply_divide_fusion.2
  367.7 2.1 dynamic-slice_negate_fusion.2
  369.8 1.7 constant_dynamic-slice_fusion.12
  371.6 4.6 %fusion.57 = f32[64,9,64,128]{3,2,1,0:T(8,128)} fusion(f32[64,9,64,128]{3,2,1,0:T(8,128)} %get-tuple-element.177, s32[]{:T(128)} %get-tuple-element.176, f32[64,64,64]{2,1,0:T(8,128)S(1)} %multiply_divide_fusion.2, bf16[64,64,128]{2,1,0:T(8,128)(2,1)S(1)} %get-tuple-element.163, bf16[64,64,128]{2,1,0:T(8,128)(2,1)S(1)} %get-tuple-element.164, ...), kind=kOutput, calls=%fused_computation.8.clone.1 | convolution fusion | flops 282066944 | bytes 9437700 | tf_op jit(solution)/shard_map/while/body/eval_jaxpr/cif,cjf->cij/dot_general | solution.py:106
  376.2 0.6 constant_dynamic-slice_fusion.10
  378.8 0.8 multiply_divide_fusion.2
  379.6 2.1 dynamic-slice_negate_fusion.2
  381.7 1.7 constant_dynamic-slice_fusion.12
  383.5 4.6 %fusion.57 = f32[64,9,64,128]{3,2,1,0:T(8,128)} fusion(f32[64,9,64,128]{3,2,1,0:T(8,128)} %get-tuple-element.177, s32[]{:T(128)} %get-tuple-element.176, f32[64,64,64]{2,1,0:T(8,128)S(1)} %multiply_divide_fusion.2, bf16[64,64,128]{2,1,0:T(8,128)(2,1)S(1)} %get-tuple-element.163, bf16[64,64,128]{2,1,0:T(8,128)(2,1)S(1)} %get-tuple-element.164, ...), kind=kOutput, calls=%fused_computation.8.clone.1 | convolution fusion | flops 282066944 | bytes 9437700 | tf_op jit(solution)/shard_map/while/body/eval_jaxpr/cif,cjf->cij/dot_general | solution.py:106
  388.1 0.6 constant_dynamic-slice_fusion.10
  390.7 0.8 multiply_divide_fusion.2
  391.6 2.1 dynamic-slice_negate_fusion.2
  393.7 1.7 constant_dynamic-slice_fusion.12
  395.4 4.6 %fusion.57 = f32[64,9,64,128]{3,2,1,0:T(8,128)} fusion(f32[64,9,64,128]{3,2,1,0:T(8,128)} %get-tuple-element.177, s32[]{:T(128)} %get-tuple-element.176, f32[64,64,64]{2,1,0:T(8,128)S(1)} %multiply_divide_fusion.2, bf16[64,64,128]{2,1,0:T(8,128)(2,1)S(1)} %get-tuple-element.163, bf16[64,64,128]{2,1,0:T(8,128)(2,1)S(1)} %get-tuple-element.164, ...), kind=kOutput, calls=%fused_computation.8.clone.1 | convolution fusion | flops 282066944 | bytes 9437700 | tf_op jit(solution)/shard_map/while/body/eval_jaxpr/cif,cjf->cij/dot_general | solution.py:106
  400.0 0.6 constant_dynamic-slice_fusion.10
  402.7 0.8 multiply_divide_fusion.2
  403.5 2.1 dynamic-slice_negate_fusion.2
  405.6 1.7 constant_dynamic-slice_fusion.12
  407.4 4.6 %fusion.57 = f32[64,9,64,128]{3,2,1,0:T(8,128)} fusion(f32[64,9,64,128]{3,2,1,0:T(8,128)} %get-tuple-element.177, s32[]{:T(128)} %get-tuple-element.176, f32[64,64,64]{2,1,0:T(8,128)S(1)} %multiply_divide_fusion.2, bf16[64,64,128]{2,1,0:T(8,128)(2,1)S(1)} %get-tuple-element.163, bf16[64,64,128]{2,1,0:T(8,128)(2,1)S(1)} %get-tuple-element.164, ...), kind=kOutput, calls=%fused_computation.8.clone.1 | convolution fusion | flops 282066944 | bytes 9437700 | tf_op jit(solution)/shard_map/while/body/eval_jaxpr/cif,cjf->cij/dot_general | solution.py:106
  412.0 0.6 constant_dynamic-slice_fusion.10
  414.6 0.8 multiply_divide_fusion.2
  415.4 2.1 dynamic-slice_negate_fusion.2
  417.5 1.7 constant_dynamic-slice_fusion.12
  419.3 4.6 %fusion.57 = f32[64,9,64,128]{3,2,1,0:T(8,128)} fusion(f32[64,9,64,128]{3,2,1,0:T(8,128)} %get-tuple-element.177, s32[]{:T(128)} %get-tuple-element.176, f32[64,64,64]{2,1,0:T(8,128)S(1)} %multiply_divide_fusion.2, bf16[64,64,128]{2,1,0:T(8,128)(2,1)S(1)} %get-tuple-element.163, bf16[64,64,128]{2,1,0:T(8,128)(2,1)S(1)} %get-tuple-element.164, ...), kind=kOutput, calls=%fused_computation.8.clone.1 | convolution fusion | flops 282066944 | bytes 9437700 | tf_op jit(solution)/shard_map/while/body/eval_jaxpr/cif,cjf->cij/dot_general | solution.py:106
  426.5 0.8 multiply_divide_fusion.2
  427.4 2.1 dynamic-slice_negate_fusion.2
  429.5 1.7 constant_dynamic-slice_fusion.12
  431.2 4.6 %fusion.57 = f32[64,9,64,128]{3,2,1,0:T(8,128)} fusion(f32[64,9,64,128]{3,2,1,0:T(8,128)} %get-tuple-element.177, s32[]{:T(128)} %get-tuple-element.176, f32[64,64,64]{2,1,0:T(8,128)S(1)} %multiply_divide_fusion.2, bf16[64,64,128]{2,1,0:T(8,128)(2,1)S(1)} %get-tuple-element.163, bf16[64,64,128]{2,1,0:T(8,128)(2,1)S(1)} %get-tuple-element.164, ...), kind=kOutput, calls=%fused_computation.8.clone.1 | convolution fusion | flops 282066944 | bytes 9437700 | tf_op jit(solution)/shard_map/while/body/eval_jaxpr/cif,cjf->cij/dot_general | solution.py:106
  435.8 0.7 copy-done.1
  (31 shorter events, 3.9 us)
Async XLA Ops:
  6.5 111.4 %copy-start = (s32[144,2]{0,1:T(2,128)S(1)}, s32[144,2]{0,1:T(2,128)}, u32[]{:S(2)}) copy-start(s32[144,2]{0,1:T(2,128)} %param.5) | copy-start | bytes 3460
  6.5 310.0 %all-gather.2.cloned.1.call-start = ((), (), s32[]{:S(2)}) async-start(), calls=%async_computation.2 | async-start | bytes 35651584 | tf_op jit(solution)/shard_map/all_gather | solution.py:118
  11.1 2.0 copy-start.2
  14.3 44.4 %collective-permute-start = (bf16[64,3,2048]{2,0,1:T(8,128)(2,1)S(1)}, bf16[64,3,2048]{2,0,1:T(8,128)(2,1)S(1)}, u32[]{:S(2)}, u32[]{:S(2)}) collective-permute-start(bf16[64,3,2048]{2,0,1:T(8,128)(2,1)S(1)} %copy.19), channel_id=1, source_target_pairs={{16,0},{32,16},{48,32},{64,48},{80,64},{96,80},{112,96},{17,1},{33... | collective-permute-start | bytes 2359304 | tf_op jit(solution)/shard_map/ppermute | solution.py:17
  56.0 3.7 copy-start.3
  59.8 5.0 %copy-start.4 = (bf16[2048,1024]{0,1:T(8,128)(2,1)S(1)}, bf16[2048,1024]{0,1:T(8,128)(2,1)}, u32[]{:S(2)}) copy-start(bf16[2048,1024]{0,1:T(8,128)(2,1)} %convert_element_type.68) | copy-start | bytes 12582916
  435.8 0.7 copy-start.1
Sparse Core Ops, SparseCore 0:
  118.0 198.4 all-gather.1
where the time goes:
time: 445 us; the launch traced here: 443 us
  waiting for transfers between devices  199 us (45%)
  local copies, waits for them, and re-layouts  66.6 us (15%)
  other arithmetic  62.7 us (14%)
  matrix products  46.3 us (10%)
  blocking collectives  34.6 us (8%)
  loops' own time  17.5 us (4%)
  between operations  13.6 us (3%)
    all_gather x1, waiting for transfers between devices, on_device(): everything = lax.all_gather(own, 'inp', axis=1, tiled=True)  198 us
    dot_general x9, matrix products, make_tile(): jnp.einsum('cif,cjf->cij', left_rows, partner, preferred_element_type=jnp...  41.6 us
    all_to_all x2, blocking collectives, exchange_in_order(): whole = lax.all_to_all(whole, axes[k], k, k, tiled=True)  34.6 us
    neg x9, other arithmetic, rotate_parts(): -rows[..., half_width:]  18.8 us
    another operation x1, loops' own time, on_device(): return lax.fori_loop(0, slot_total, place, outputs)  17.5 us
    another operation x1, other arithmetic  17.1 us
    dynamic_slice x9, local copies, waits for them, and re-layouts, make_tile(): lax.dynamic_slice_in_dim(everything, second * block_width, block_width, 1)  15.7 us
    reduce_sum x1, other arithmetic, on_device(): jnp.sum(jnp.square(everything.astype(jnp.float32)), axis=2) / frame_total  11.9 us
  transfers between devices with their start and end apart: 2, of which 1 were waited for; matrix products, arithmetic and copies ran while one was open for 9% of the time, Pallas kernels for 0%

commit v1 on v0

--- a/solution.py
+++ b/solution.py
@@ -115,7 +115,8 @@
     spectra = channelize(voltages)
     turned = core_and_chips(spectra, ("chan_0", "chan_1"), (1, 0), 2, 1)
     own = arrange(turned)
-    everything = lax.all_gather(own, "inp", axis=1, tiled=True)
+    sent = jnp.stack([own] * lax.axis_size("inp"))
+    everything = jnp.concatenate(lax.all_to_all(sent, "inp", 0, 0), axis=1)
     frame_total = everything.shape[2] // 2
     autopower = jnp.sum(jnp.square(everything.astype(jnp.float32)), axis=2) / frame_total + 1e-06
     slot_total = tile_table.shape[0] // lax.axis_size("inp")

time: 445 us -> 769 us (1.73)
  waiting for transfers between devices: 199 us -> 495 us
  local copies, waits for them, and re-layouts: 66.6 us -> 99.5 us
  between operations: 13.6 us -> 0.21 us
    all_to_all x0 -> x1, waiting for transfers between devices: none -> 495 us  [on_device(): everything = jnp.concatenate(lax.all_to_all(sent, 'inp', 0, 0), axis=1)]
    all_gather x1 -> x0, waiting for transfers between devices: 198 us -> none  [on_device(): everything = lax.all_gather(own, 'inp', axis=1, tiled=True)]
    all_to_all x0 -> x1, local copies, waits for them, and re-layouts: none -> 22.9 us  [on_device(): everything = jnp.concatenate(lax.all_to_all(sent, 'inp', 0, 0), axis=1)]
    another operation x0 -> x2, local copies, waits for them, and re-layouts: none -> 14.7 us  [on_device(): sent = jnp.stack([own] * lax.axis_size('inp'))]
  transfers between devices with their start and end apart: 2 -> 2, of which waited for: 1 -> 1; matrix products, arithmetic and copies ran while one was open for 9% -> 5% of each run, Pallas kernels for 0% -> 0%
where the time goes in v1:
time: 769 us; the launch traced here: 766 us
  waiting for transfers between devices  495 us (64%)
  local copies, waits for them, and re-layouts  99.5 us (13%)
  other arithmetic  62.7 us (8%)
  matrix products  46.4 us (6%)
  blocking collectives  34.6 us (4%)
  loops' own time  16.5 us (2%)
  starting transfers between devices  11.1 us (1%)
    all_to_all x1, waiting for transfers between devices, on_device(): everything = jnp.concatenate(lax.all_to_all(sent, 'inp', 0, 0), axis=1)  495 us
    dot_general x9, matrix products, make_tile(): jnp.einsum('cif,cjf->cij', left_rows, partner, preferred_element_type=jnp...  41.6 us
    all_to_all x2, blocking collectives, exchange_in_order(): whole = lax.all_to_all(whole, axes[k], k, k, tiled=True)  34.6 us
    all_to_all x1, local copies, waits for them, and re-layouts, on_device(): everything = jnp.concatenate(lax.all_to_all(sent, 'inp', 0, 0), axis=1)  22.9 us
    neg x9, other arithmetic, rotate_parts(): -rows[..., half_width:]  18.8 us
    another operation x1, other arithmetic  17.1 us
    another operation x1, loops' own time, on_device(): return lax.fori_loop(0, slot_total, place, outputs)  16.5 us
    dynamic_slice x9, local copies, waits for them, and re-layouts, make_tile(): lax.dynamic_slice_in_dim(everything, second * block_width, block_width, 1)  15.7 us
  transfers between devices with their start and end apart: 2, of which 1 were waited for; matrix products, arithmetic and copies ran while one was open for 5% of the time, Pallas kernels for 0%

profile of v1, /device:TPU:1, one launch (start us, length us, event | category | flops | bytes accessed | tf_op | source)
XLA Modules:
  0.0 766.0 jit_solution(9282711150781596483)
XLA Ops:
  0.0 4.6 copy.33
  4.6 2.0 copy-done.2
  7.7 3.5 collective-permute-start
  11.2 17.1 %negate_convert_fusion = (bf16[2048,512,1]{1,0,2:T(8,128)(2,1)S(1)}, bf16[2048,512,1]{1,0,2:T(8,128)(2,1)S(1)}) fusion(), kind=kLoop, calls=%fused_computation.29 | loop fusion | flops 17825792 | bytes 4194304 | tf_op jit(solution)/shard_map/convert.2
  28.4 2.3 pad_maximum_fusion
  30.7 11.3 %copy.22 = bf16[2048,512,2]{0,2,1:T(2,128)(2,1)} copy(bf16[2048,512,2]{1,0,2:T(8,128)(2,1)} %pad_maximum_fusion) | data formatting | bytes 8388608 | tf_op jit(solution)/shard_map/stack | solution.py:58
  42.0 7.3 convert_element_type.69
  49.5 2.7 constant_dynamic-update-slice_fusion
  52.1 1.0 copy_dynamic-update-slice_fusion
  53.2 5.0 add_convert_fusion
  58.2 4.8 convert_bitcast_fusion
  64.2 5.1 all_to_all.15
  69.7 29.6 %all_to_all.16 = bf16[4,2,64,16,128]{4,3,2,1,0:T(8,128)(2,1)S(1)} all-to-all(bf16[4,2,64,16,128]{4,3,2,1,0:T(8,128)(2,1)S(1)} %copy.25), channel_id=1, replica_groups=mesh['chan_0'=4,'chan_1'=2,'inp'=16] {'chan_0'}, dimensions={0} | all-to-all | bytes 4194304 | tf_op jit(solution)/shard_map/all_to_all | solution.py:35
  99.2 7.4 copy.26
  106.6 3.5 copy.27
  110.1 11.1 %stack.10 = bf16[16,64,64,256]{3,2,1,0:T(8,128)(2,1)} broadcast(bf16[64,64,256]{2,1,0:T(8,128)(2,1)S(1)} %copy.27), dimensions={1,2,3} | broadcast | bytes 35651584 | tf_op jit(solution)/shard_map/stack | solution.py:118
  121.2 7.6 all-to-all-start.2
  129.0 494.9 %all-to-all-done.2 = bf16[16,64,64,256]{3,2,1,0:T(8,128)(2,1)} async-done(((bf16[16,64,64,256]{3,2,1,0:T(8,128)(2,1)}), bf16[16,64,64,256]{3,2,1,0:T(8,128)(2,1)}, u32[]{:S(2)}, u32[]{:S(2)}) %all-to-all-start.2) | async-done | bytes 33554464 | tf_op jit(solution)/shard_map/all_to_all | solution.py:119
  623.9 11.8 %multiply_reduce_fusion = f32[64,16,64]{2,1,0:T(8,128)S(1)} fusion(bf16[16,64,64,256]{3,2,1,0:T(8,128)(2,1)} %all-to-all-done.2), kind=kLoop, calls=%fused_computation.20 | loop fusion | flops 50266112 | bytes 33816576 | tf_op jit(solution)/shard_map/reduce_sum | solution.py:121
  636.0 22.9 %copy.28 = bf16[16,64,64,256]{3,2,0,1:T(8,128)(2,1)} copy(bf16[16,64,64,256]{3,2,1,0:T(8,128)(2,1)} %all-to-all-done.2) | data formatting | bytes 67108864 | tf_op jit(solution)/shard_map/all_to_all | solution.py:119
  658.9 106.4 %while.13 = (s32[]{:T(128)}, f32[64,9,64,128]{3,2,1,0:T(8,128)}, s32[9,2]{0,1:T(2,128)S(1)}, bf16[64,1024,256]{2,1,0:T(8,128)(2,1)}, f32[64,1024]{1,0:T(8,128)S(...) while((s32[]{:T(128)}, f32[64,9,64,128]{3,2,1,0:T(8,128)}, ...), condition=%wide.region_2.3_spmd, body=%wide.region_1.2_spmd.sunk | while | flops 284426240 | bytes 18973484 | solution.py:140
  658.9 0.6 constant_dynamic-slice_fusion.10
  661.5 0.8 multiply_divide_fusion.2
  662.3 2.1 dynamic-slice_negate_fusion.2
  664.4 1.7 constant_dynamic-slice_fusion.12
  666.1 4.6 fusion.57
  670.8 0.6 constant_dynamic-slice_fusion.10
  673.3 0.8 multiply_divide_fusion.2
  674.1 2.1 dynamic-slice_negate_fusion.2
  676.2 1.7 constant_dynamic-slice_fusion.12
  678.0 4.6 fusion.57
  682.6 0.6 constant_dynamic-slice_fusion.10
  685.1 0.8 multiply_divide_fusion.2
  685.9 2.1 dynamic-slice_negate_fusion.2
  688.0 1.7 constant_dynamic-slice_fusion.12
  689.8 4.6 fusion.57
  694.4 0.6 constant_dynamic-slice_fusion.10
  696.9 0.8 multiply_divide_fusion.2
  697.8 2.1 dynamic-slice_negate_fusion.2
  699.9 1.7 constant_dynamic-slice_fusion.12
  701.6 4.6 fusion.57
  706.2 0.6 constant_dynamic-slice_fusion.10
  708.7 0.8 multiply_divide_fusion.2
  709.6 2.1 dynamic-slice_negate_fusion.2
  711.7 1.7 constant_dynamic-slice_fusion.12
  713.4 4.6 fusion.57
  720.6 0.8 multiply_divide_fusion.2
  721.4 2.1 dynamic-slice_negate_fusion.2
  723.5 1.7 constant_dynamic-slice_fusion.12
  725.3 4.6 fusion.57
  729.9 0.6 constant_dynamic-slice_fusion.10
  732.4 0.8 multiply_divide_fusion.2
  733.2 2.1 dynamic-slice_negate_fusion.2
  735.3 1.7 constant_dynamic-slice_fusion.12
  737.1 4.6 fusion.57
  744.2 0.8 multiply_divide_fusion.2
  745.1 2.1 dynamic-slice_negate_fusion.2
  747.2 1.7 constant_dynamic-slice_fusion.12
  748.9 4.6 fusion.57
  756.0 0.8 multiply_divide_fusion.2
  756.9 2.1 dynamic-slice_negate_fusion.2
  759.0 1.7 constant_dynamic-slice_fusion.12
  760.7 4.6 fusion.57
  765.3 0.7 copy-done.1
  (33 shorter events, 5.9 us)
Async XLA Ops:
  0.0 128.9 %copy-start = (s32[144,2]{0,1:T(2,128)S(1)}, s32[144,2]{0,1:T(2,128)}, u32[]{:S(2)}) copy-start(s32[144,2]{0,1:T(2,128)} %param.5) | copy-start | bytes 3460
  4.6 2.0 copy-start.2
  7.7 44.4 %collective-permute-start = (bf16[64,3,2048]{2,0,1:T(8,128)(2,1)S(1)}, bf16[64,3,2048]{2,0,1:T(8,128)(2,1)S(1)}, u32[]{:S(2)}, u32[]{:S(2)}) collective-permute-start(bf16[64,3,2048]{2,0,1:T(8,128)(2,1)S(1)} %copy.20), channel_id=1, source_target_pairs={{16,0},{32,16},{48,32},{64,48},{80,64},{96,80},{112,96},{17,1},{33... | collective-permute-start | bytes 2359304 | tf_op jit(solution)/shard_map/ppermute | solution.py:17
  49.5 3.7 copy-start.3
  53.2 5.0 copy-start.4
  121.2 502.7 %all-to-all-start.2 = ((bf16[16,64,64,256]{3,2,1,0:T(8,128)(2,1)}), bf16[16,64,64,256]{3,2,1,0:T(8,128)(2,1)}, u32[]{:S(2)}, u32[]{:S(2)}) async-start(bf16[16,64,64,256]{3,2,1,0:T(8,128)(2,1)} %stack.10), calls=%async_computation.2 | async-start | bytes 67108864 | tf_op jit(solution)/shard_map/all_to_all | solution.py:119
  765.3 0.7 copy-start.1
